TPU v7x, 32 devices: a whole 2x2x4 slice. The times are simulated.
32 devices in a mesh: groups: 2 (over y), owner: 4 (over z), sub: 2 (over x), pair: 2 (over core).
Axes of the slice: x: 2, y: 2, z: 4, core: 2. Of those that a mesh axis runs over, the one named last changes fastest.
Arguments:
- embeddings: float32 [16, 2, 128, 1152], P(('groups', 'owner', 'sub'), 'pair'), parts along dimension 0, may hold values from -12 to 12
- moves: int32 [2, 16, 2, 128], P(None, ('groups', 'owner', 'sub'), 'pair'), parts along dimension 1, may hold values from -1 to 7, as said below
Outputs:
- curated: float32 [16, 2, 128, 1152], P(('groups', 'owner', 'sub'), 'pair'), parts along dimension 0
There are 2 independent parts, one for each index of `groups`. A program takes and returns all parts, laid end to end along the dimension named above; each array names one. Nothing has to cross between parts.
Inputs may be any that keep to these rules, and one draw needn't show every extreme that they name: moves[m, c, p, s] is the cluster to which the row in slot s of device (c, p) goes after pass m + 1, or -1 for an empty slot; the row stays on pair index p. A device's live slots come first. In one list at most 16 live rows of one device go to one cluster, and some device sends 16 to every cluster; some device holds 128 live rows and some device receives 128, in every list. The live slots of a device in list m + 1 number exactly the rows it receives from list m.
All inputs are finite; a program needn't handle non-finite values.
Results may differ from a plain program's by a relative error of at most 0.002.
Values may be sent and summed in bfloat16 or wider, within the bound.
No kernel may reach another device: no remote copies, remote signals or barrier semaphores. Data moves between devices by JAX's collectives and lax.ppermute only.
A program may use at most 64 MiB of HBM per device.

v0:
```python
import jax
import jax.numpy as jnp
from jax import lax
from jax.experimental import pallas as pl
from jax.experimental.pallas import tpu as pltpu
from jax.sharding import PartitionSpec as P


PASSES = 3
SHARES = 2
LANES = 128
MARK = 2.0
CHUNKS = 4


epsilon = 1e-06
sharpness = 6.0

f32 = jnp.float32
bf16 = jnp.bfloat16
i32 = jnp.int32


def offset_of(clusters, step, core):
    return clusters - 1 - 2 * step - (core ^ (step & 1))


def here():
    cluster = lax.axis_index("owner") * lax.axis_size("sub") + lax.axis_index("sub")
    return cluster, lax.axis_index("pair")


def iota(shape, axis):
    return lax.broadcasted_iota(i32, shape, axis)


def mark_empty(head, live):
    return jnp.where((iota(head.shape, 1) == 0) & jnp.logical_not(live), MARK, head)


def unit_rows(values, targets):
    count = jnp.sum((targets >= 0).astype(f32), axis=1, keepdims=True)
    live = iota((values.shape[0], 1), 0).astype(f32) < count
    total = jnp.sum(values * values, axis=1, keepdims=True)
    unit = jnp.where(live, values * lax.rsqrt(total + epsilon), 0.0).astype(bf16)
    flags = jnp.broadcast_to(live.astype(f32), (values.shape[0], LANES)).astype(bf16)
    return unit, flags


def state_kernel(emb_ref, moves_ref, out_ref, flags_ref):
    out_ref[...], flags_ref[...] = unit_rows(emb_ref[...], moves_ref[0:1, :])


def index_kernel(clusters, most, own_ref, peer_ref, wanted_ref, ahead_ref):
    lists, rows = own_ref.shape
    cluster, core = here()
    before = (iota((rows, rows), 0) < iota((rows, rows), 1)).astype(bf16)
    for number in range(lists):
        for half, ref in enumerate((own_ref, peer_ref)):
            targets = ref[number : number + 1, :]
            onehot = (iota((clusters, rows), 0) == targets).astype(f32)
            earlier = jnp.dot(onehot.astype(bf16), before, preferred_element_type=f32)
            rank = jnp.sum(onehot * earlier, axis=0, keepdims=True).astype(i32)
            back = clusters - 1 - (targets ^ cluster)
            step = back >> 1
            mine = ((back & 1) ^ (step & 1)) == core
            place = (step * SHARES + (core ^ half)) * most + rank
            place = jnp.where((targets >= 0) & mine, place, -1)
            wanted_ref[number, :, half * rows : (half + 1) * rows] = (
                iota((rows, rows), 0) == place
            ).astype(bf16)
    _, key = arrival(clusters, most, rows, iota((SHARES * rows, 1), 0))
    _, other = arrival(clusters, most, rows, iota((1, SHARES * rows), 1))
    ahead = key - other
    ahead_ref[...] = ((ahead > 0) & (ahead < 2 * rows)).astype(bf16)


def arrival(clusters, most, rows, index):
    cluster, core = here()
    half = (index >= rows).astype(i32)
    inner = index - half * rows
    step = inner // (SHARES * most)
    share = (inner // most) & 1
    source = cluster ^ offset_of(clusters, step, core ^ half)
    return share, share * (4 * rows) + source * most + inner % most


def pass_kernel(clusters, most, number, last, count, *refs):
    blocks, outs = refs[:count], refs[count + 2 :]
    wanted_ref, ahead_ref = refs[count : count + 2]
    width = blocks[0].shape[1]
    total_rows = ahead_ref.shape[0]
    rows = total_rows // SHARES

    if number == 0:
        state_ref, flags_ref, peer_ref, targets_ref = blocks
        peer, peer_flags = unit_rows(peer_ref[...], targets_ref[0:1, :])
        keys = jnp.concatenate([state_ref[...], peer], axis=0)
        flags = jnp.concatenate([flags_ref[...], peer_flags], axis=0)
        scores = lax.dot_general(keys, keys, (((1,), (1,)), ((), ())), preferred_element_type=f32)
        select = wanted_ref[number]
    else:
        heads = jnp.concatenate([ref[:, :LANES] for ref in blocks], axis=0).astype(f32)
        live = jnp.broadcast_to((heads[:, 0:1] < 1.5).astype(f32), (total_rows, LANES))
        heads = jnp.where(live > 0.5, heads, 0.0).astype(bf16)
        tails = jnp.concatenate([ref[:, LANES:] for ref in blocks], axis=0)
        keys = jnp.concatenate([heads, tails], axis=1)
        flags = live.astype(bf16)
        rough = jnp.concatenate([ref[...] for ref in blocks], axis=0)
        scores = lax.dot_general(rough, rough, (((1,), (1,)), ((), ())), preferred_element_type=f32)
        _, core = here()
        share, _ = arrival(clusters, most, rows, iota((total_rows, 1), 0))
        slot = jnp.dot(ahead_ref[...], flags, preferred_element_type=f32)
        slot = jnp.where(live > 0.5, slot, -1.0)[:, 0:1]
        lane = iota((total_rows, rows), 1).astype(f32)
        own = (share == core).astype(f32)
        mine = ((slot == lane) & (own > 0.5)).astype(bf16)
        if last:
            wanted = (iota((rows, rows), 0) == iota((rows, rows), 1)).astype(bf16)
        else:
            theirs = ((slot == lane) & (own < 0.5)).astype(bf16)
            mine = jnp.concatenate([mine, theirs], axis=1)
            wanted = wanted_ref[number]
        select = lax.dot_general(
            wanted, mine, (((1,), (1,)), ((), ())), preferred_element_type=f32
        ).astype(bf16)

    weights = jnp.exp(sharpness * (scores - 1.0)).astype(bf16)
    chosen = jnp.dot(select, weights, preferred_element_type=f32).astype(bf16)
    sums = jnp.dot(
        chosen, jnp.concatenate([keys, flags], axis=1), preferred_element_type=f32
    )
    numer = sums[:, :width]
    denom = sums[:, width : width + 1]
    found = denom > 0.0
    inverse = 1.0 / jnp.where(found, denom, 1.0)
    total = jnp.sum(numer * numer, axis=1, keepdims=True)
    scale = inverse * lax.rsqrt(total * (inverse * inverse) + epsilon)
    if last:
        out, staged, done = outs
        size = rows // CHUNKS
        copies = []
        for index in range(CHUNKS):
            part = slice(index * size, (index + 1) * size)
            staged[part] = jnp.where(found[part], numer[part] * scale[part], 0.0)
            copies.append(pltpu.make_async_copy(staged.at[part], out.at[part], done.at[index]))
            copies[-1].start()
        for copy in copies:
            copy.wait()
        return
    unit = jnp.where(found, numer * scale, 0.0)
    head = mark_empty(unit[:, :LANES], found).astype(bf16)
    tail = unit[:, LANES:].astype(bf16)
    size = outs[0].shape[0]
    for index, out in enumerate(outs):
        out[:, :LANES] = head[index * size : (index + 1) * size]
        out[:, LANES:] = tail[index * size : (index + 1) * size]


def call(kernel, out, *args, space=pltpu.VMEM, scratch=()):
    return pl.pallas_call(
        kernel,
        out_shape=out,
        in_specs=[pl.BlockSpec(memory_space=pltpu.VMEM)] * len(args),
        out_specs=jax.tree.map(lambda _: pl.BlockSpec(memory_space=space), out),
        scratch_shapes=scratch,
        compiler_params=pltpu.CompilerParams(vmem_limit_bytes=16 * 2**20),
    )(*args)


def swap_pair(values):
    return lax.ppermute(values, "pair", [(0, 1), (1, 0)])


def send(values, clusters, step):
    pairs = [
        (cluster * 2 + core, (cluster ^ offset_of(clusters, step, core)) * 2 + core)
        for cluster in range(clusters)
        for core in range(2)
    ]
    return lax.ppermute(values, ("owner", "sub", "pair"), pairs)


def body(embeddings, moves):
    rows, width = embeddings.shape[2:]
    clusters = lax.axis_size("owner") * lax.axis_size("sub")
    most = rows // clusters
    steps = clusters // 2
    block = SHARES * most
    aligned = block % 16 == 0
    targets = moves[:, 0, 0, :]
    values = embeddings[0, 0]
    peer_targets = swap_pair(targets)
    peer_values = swap_pair(values)
    state, flags = call(
        state_kernel,
        [
            jax.ShapeDtypeStruct((rows, width), bf16),
            jax.ShapeDtypeStruct((rows, LANES), bf16),
        ],
        values,
        targets,
    )
    tables = call(
        lambda *refs: index_kernel(clusters, most, *refs),
        [
            jax.ShapeDtypeStruct((targets.shape[0], rows, SHARES * rows), bf16),
            jax.ShapeDtypeStruct((SHARES * rows, SHARES * rows), bf16),
        ],
        targets,
        peer_targets,
    )
    keys = [state, flags, peer_values, peer_targets]
    for number in range(PASSES):
        last = number + 1 == PASSES
        if last:
            out = jax.ShapeDtypeStruct((rows, width), f32)
        elif aligned:
            out = [jax.ShapeDtypeStruct((block, width), bf16)] * steps
        else:
            out = [jax.ShapeDtypeStruct((rows, width), bf16)]
        result = call(
            lambda *refs: pass_kernel(clusters, most, number, last, len(keys), *refs),
            out,
            *keys,
            *tables,
            space=pl.ANY if last else pltpu.VMEM,
            scratch=[pltpu.VMEM((rows, width), f32), pltpu.SemaphoreType.DMA((CHUNKS,))]
            if last
            else (),
        )
        if last:
            return result[None, None]
        if not aligned:
            result = [result[0][step * block : (step + 1) * block] for step in range(steps)]
        far, near = [], []
        for step in range(steps):
            far.append(send(result[step], clusters, step))
        for step in range(steps):
            near.append(swap_pair(far[step]))
        if aligned:
            keys = far + near
        else:
            keys = [jnp.concatenate(far, axis=0), jnp.concatenate(near, axis=0)]


def solution(mesh):
    placed = (
        P(("groups", "owner", "sub"), "pair", None, None),
        P(None, ("groups", "owner", "sub"), "pair", None),
    )
    return jax.shard_map(
        body,
        mesh=mesh,
        in_specs=placed,
        out_specs=P(("groups", "owner", "sub"), "pair", None, None),
        check_vma=False,
    )
```

profile of v0, /device:TPU:0, one launch (start us, length us, event | category | flops | bytes accessed | tf_op | source)
XLA Modules:
  0.0 32.5 jit_solution(2248530447760149820)
XLA Ops:
  0.0 0.0 copy-start.1
  0.0 0.5 %collective-permute-start = (f32[128,1152]{1,0:T(8,128)}, f32[128,1152]{1,0:T(8,128)S(1)}, u32[]{:S(2)}, u32[]{:S(2)}) collective-permute-start(f32[128,1152]{1,0:T(8,128)} %bitcast.3), channel_id=1, source_target_pairs={{0,1},{1,0},{2,3},{3,2},{4,5},{5,4},{6,7},{7,6},{8,9},{9,8},{10,11... | collective-permute-start | bytes 1769480 | tf_op jit(solution)/shard_map/ppermute | solution.py:172
  0.5 0.2 copy-done.1
  0.7 0.5 %collective-permute-start.1 = (s32[2,128]{1,0:T(2,128)S(1)}, s32[2,128]{1,0:T(2,128)S(1)}, u32[]{:S(2)}, u32[]{:S(2)}) collective-permute-start(s32[2,128]{1,0:T(2,128)S(1)} %bitcast.5), channel_id=1, source_target_pairs={{0,1},{1,0},{2,3},{3,2},{4,5},{5,4},{6,7},{7,6},{8,9},{9,8},{10,11... | collective-permute-start | bytes 3080 | tf_op jit(solution)/shard_map/ppermute | solution.py:172
  1.2 0.0 copy-start
  1.2 1.1 %copy-done = f32[1,1,128,1152]{3,2,1,0:T(8,128)S(1)} copy-done((f32[1,1,128,1152]{3,2,1,0:T(8,128)S(1)}, f32[1,1,128,1152]{3,2,1,0:T(8,128)}, u32[]{:S(2)}) %copy-start) | copy-done | bytes 589848
  2.2 0.2 shard_map.28
  2.4 0.0 collective-permute-done.1.refs_1_.refs_3_
  2.4 0.3 shard_map.29
  2.7 0.0 collective-permute-done.refs_2_
  2.7 1.2 %shard_map.30 = (bf16[32,1152]{1,0:T(8,128)(2,1)S(1)}, bf16[32,1152]{1,0:T(8,128)(2,1)S(1)}, bf16[32,1152]{1,0:T(8,128)(2,1)S(1)}, bf16[32,1152]{1,0:T(8,128)(2,1)S(1)}) custom-call(bf16[128,1152]{1,0:T(8,128)(2,1)S(1)} %get-tuple-element.17.refs_0_, bf16[128,128]{1,0:T(8,128)(2,1)S(1)} %get-tuple-element.18.refs_1_, ...), custom_call_target="tpu_custom_call" | custom-call | tf_op jit(solution)/shard_map/pallas_call | solution.py:161
  3.9 5.9 %collective-permute-start.2 = (bf16[32,1152]{1,0:T(8,128)(2,1)S(1)}, bf16[32,1152]{1,0:T(8,128)(2,1)S(1)}, u32[]{:S(2)}, u32[]{:S(2)}) collective-permute-start(bf16[32,1152]{1,0:T(8,128)(2,1)S(1)} %get-tuple-element.21), channel_id=1, source_target_pairs={{0,14},{1,13},{2,12},{3,15},{4,10},{5,9},{6,8},{7,11},{8,6},{9,5},... | collective-permute-start | bytes 221192 | tf_op jit(solution)/shard_map/ppermute | solution.py:181
  9.8 0.0 collective-permute-start.3
  9.8 0.6 %collective-permute-start.4 = (bf16[32,1152]{1,0:T(8,128)(2,1)S(1)}, bf16[32,1152]{1,0:T(8,128)(2,1)S(1)}, u32[]{:S(2)}, u32[]{:S(2)}) collective-permute-start(bf16[32,1152]{1,0:T(8,128)(2,1)S(1)} %get-tuple-element.23), channel_id=1, source_target_pairs={{0,6},{1,5},{2,4},{3,7},{4,2},{5,1},{6,0},{7,3},{8,14},{9,13},{10,... | collective-permute-start | bytes 221192 | tf_op jit(solution)/shard_map/ppermute | solution.py:181
  10.4 0.7 %collective-permute-start.5 = (bf16[32,1152]{1,0:T(8,128)(2,1)S(1)}, bf16[32,1152]{1,0:T(8,128)(2,1)S(1)}, u32[]{:S(2)}, u32[]{:S(2)}) collective-permute-start(bf16[32,1152]{1,0:T(8,128)(2,1)S(1)} %get-tuple-element.24), channel_id=1, source_target_pairs={{0,0},{1,3},{2,2},{3,1},{4,4},{5,7},{6,6},{7,5},{8,8},{9,11},{10,1... | collective-permute-start | bytes 221192 | tf_op jit(solution)/shard_map/ppermute | solution.py:181
  11.1 1.8 %collective-permute-done.2.refs_0_ = bf16[32,1152]{1,0:T(8,128)(2,1)S(1)} collective-permute-done((bf16[32,1152]{1,0:T(8,128)(2,1)S(1)}, bf16[32,1152]{1,0:T(8,128)(2,1)S(1)}, u32[]{:S(2)}, u32[]{:S(2)}) %collective-permute-start.2) | collective-permute-done | bytes 73760 | tf_op jit(solution)/shard_map/ppermute | solution.py:181
  12.8 0.0 collective-permute-start.6
  12.9 2.8 %collective-permute-done.3.refs_1_ = bf16[32,1152]{1,0:T(8,128)(2,1)S(1)} collective-permute-done((bf16[32,1152]{1,0:T(8,128)(2,1)S(1)}, bf16[32,1152]{1,0:T(8,128)(2,1)S(1)}, u32[]{:S(2)}, u32[]{:S(2)}) %collective-permute-start.3) | collective-permute-done | bytes 73760 | tf_op jit(solution)/shard_map/ppermute | solution.py:181
  15.6 0.0 collective-permute-start.7
  15.6 0.9 %collective-permute-done.4.refs_2_ = bf16[32,1152]{1,0:T(8,128)(2,1)S(1)} collective-permute-done((bf16[32,1152]{1,0:T(8,128)(2,1)S(1)}, bf16[32,1152]{1,0:T(8,128)(2,1)S(1)}, u32[]{:S(2)}, u32[]{:S(2)}) %collective-permute-start.4) | collective-permute-done | bytes 73760 | tf_op jit(solution)/shard_map/ppermute | solution.py:181
  16.6 0.0 collective-permute-start.8
  16.6 0.0 collective-permute-done.5.refs_3_
  16.6 0.5 %collective-permute-start.9 = (bf16[32,1152]{1,0:T(8,128)(2,1)S(1)}, bf16[32,1152]{1,0:T(8,128)(2,1)S(1)}, u32[]{:S(2)}, u32[]{:S(2)}) collective-permute-start(bf16[32,1152]{1,0:T(8,128)(2,1)S(1)} %collective-permute-done.5.refs_3_), channel_id=1, source_target_pairs={{0,1},{1,0},{2,3},{3,2},{4,5},{5,4},{6,7},{7,6},{8,9},{9,8},{10,11... | collective-permute-start | bytes 221192 | tf_op jit(solution)/shard_map/ppermute | solution.py:172
  17.1 0.0 collective-permute-done.6.refs_4_
  17.1 0.0 collective-permute-done.7.refs_5_
  17.1 0.7 %collective-permute-done.8.refs_6_ = bf16[32,1152]{1,0:T(8,128)(2,1)S(1)} collective-permute-done((bf16[32,1152]{1,0:T(8,128)(2,1)S(1)}, bf16[32,1152]{1,0:T(8,128)(2,1)S(1)}, u32[]{:S(2)}, u32[]{:S(2)}) %collective-permute-start.8) | collective-permute-done | bytes 73760 | tf_op jit(solution)/shard_map/ppermute | solution.py:172
  17.8 0.2 collective-permute-done.9.refs_7_
  18.0 1.2 %shard_map.31 = (bf16[32,1152]{1,0:T(8,128)(2,1)S(1)}, bf16[32,1152]{1,0:T(8,128)(2,1)S(1)}, bf16[32,1152]{1,0:T(8,128)(2,1)S(1)}, bf16[32,1152]{1,0:T(8,128)(2,1)S(1)}) custom-call(bf16[32,1152]{1,0:T(8,128)(2,1)S(1)} %collective-permute-done.2.refs_0_, bf16[32,1152]{1,0:T(8,128)(2,1)S(1)} %collective-permute-done.3.refs_1_, ...), custom_call_target="tpu_custom_call" | custom-call | tf_op jit(solution)/shard_map/pallas_call | solution.py:161
  19.2 2.7 %collective-permute-start.10 = (bf16[32,1152]{1,0:T(8,128)(2,1)S(1)}, bf16[32,1152]{1,0:T(8,128)(2,1)S(1)}, u32[]{:S(2)}, u32[]{:S(2)}) collective-permute-start(bf16[32,1152]{1,0:T(8,128)(2,1)S(1)} %get-tuple-element.25), channel_id=1, source_target_pairs={{0,14},{1,13},{2,12},{3,15},{4,10},{5,9},{6,8},{7,11},{8,6},{9,5},... | collective-permute-start | bytes 221192 | tf_op jit(solution)/shard_map/ppermute | solution.py:181
  21.9 0.0 collective-permute-start.11
  21.9 2.7 %collective-permute-start.12 = (bf16[32,1152]{1,0:T(8,128)(2,1)S(1)}, bf16[32,1152]{1,0:T(8,128)(2,1)S(1)}, u32[]{:S(2)}, u32[]{:S(2)}) collective-permute-start(bf16[32,1152]{1,0:T(8,128)(2,1)S(1)} %get-tuple-element.27), channel_id=1, source_target_pairs={{0,6},{1,5},{2,4},{3,7},{4,2},{5,1},{6,0},{7,3},{8,14},{9,13},{10,... | collective-permute-start | bytes 221192 | tf_op jit(solution)/shard_map/ppermute | solution.py:181
  24.6 0.7 %collective-permute-start.13 = (bf16[32,1152]{1,0:T(8,128)(2,1)S(1)}, bf16[32,1152]{1,0:T(8,128)(2,1)S(1)}, u32[]{:S(2)}, u32[]{:S(2)}) collective-permute-start(bf16[32,1152]{1,0:T(8,128)(2,1)S(1)} %get-tuple-element.28), channel_id=1, source_target_pairs={{0,0},{1,3},{2,2},{3,1},{4,4},{5,7},{6,6},{7,5},{8,8},{9,11},{10,1... | collective-permute-start | bytes 221192 | tf_op jit(solution)/shard_map/ppermute | solution.py:181
  25.2 1.7 %collective-permute-done.10.refs_0_ = bf16[32,1152]{1,0:T(8,128)(2,1)S(1)} collective-permute-done((bf16[32,1152]{1,0:T(8,128)(2,1)S(1)}, bf16[32,1152]{1,0:T(8,128)(2,1)S(1)}, u32[]{:S(2)}, u32[]{:S(2)}) %collective-permute-start.10) | collective-permute-done | bytes 73760 | tf_op jit(solution)/shard_map/ppermute | solution.py:181
  27.0 0.0 collective-permute-start.14
  27.0 1.9 %collective-permute-done.11.refs_1_ = bf16[32,1152]{1,0:T(8,128)(2,1)S(1)} collective-permute-done((bf16[32,1152]{1,0:T(8,128)(2,1)S(1)}, bf16[32,1152]{1,0:T(8,128)(2,1)S(1)}, u32[]{:S(2)}, u32[]{:S(2)}) %collective-permute-start.11) | collective-permute-done | bytes 73760 | tf_op jit(solution)/shard_map/ppermute | solution.py:181
  28.8 0.2 collective-permute-start.15
  29.0 0.0 collective-permute-done.12.refs_2_
  29.0 0.3 collective-permute-start.16
  29.4 0.0 collective-permute-done.13.refs_3_
  29.4 0.2 collective-permute-start.17
  29.6 0.0 collective-permute-done.14.refs_4_
  29.6 0.5 %collective-permute-done.15.refs_5_ = bf16[32,1152]{1,0:T(8,128)(2,1)S(1)} collective-permute-done((bf16[32,1152]{1,0:T(8,128)(2,1)S(1)}, bf16[32,1152]{1,0:T(8,128)(2,1)S(1)}, u32[]{:S(2)}, u32[]{:S(2)}) %collective-permute-start.15) | collective-permute-done | bytes 73760 | tf_op jit(solution)/shard_map/ppermute | solution.py:172
  30.1 0.2 collective-permute-done.16.refs_6_
  30.3 0.3 collective-permute-done.17.refs_7_
  30.6 1.9 %shard_map.32 = f32[128,1152]{1,0:T(8,128)} custom-call(bf16[32,1152]{1,0:T(8,128)(2,1)S(1)} %collective-permute-done.10.refs_0_, bf16[32,1152]{1,0:T(8,128)(2,1)S(1)} %collective-permute-done.11.refs_1_, bf16[32,1152]{1,0:T(8,128)(2,1)S(1)} %collective-permute-done.12.refs_2_, bf16[32,1152]{1,0:T(8,128)(2,1)S(1)} %collective-permute-done.13.refs_3_, ...), custom_call_target="tpu_custom_call" | custom-call | tf_op jit(solution)/shard_map/pallas_call | solution.py:161
Async XLA Ops:
  0.0 0.7 %copy-start.1 = (s32[2,1,1,128]{3,2,1,0:T(1,128)S(1)}, s32[2,1,1,128]{3,2,1,0:T(1,128)}, u32[]{:S(2)}) copy-start(s32[2,1,1,128]{3,2,1,0:T(1,128)} %param.3) | copy-start | bytes 3076
  0.0 2.7 %collective-permute-start = (f32[128,1152]{1,0:T(8,128)}, f32[128,1152]{1,0:T(8,128)S(1)}, u32[]{:S(2)}, u32[]{:S(2)}) collective-permute-start(f32[128,1152]{1,0:T(8,128)} %bitcast.3), channel_id=1, source_target_pairs={{0,1},{1,0},{2,3},{3,2},{4,5},{5,4},{6,7},{7,6},{8,9},{9,8},{10,11... | collective-permute-start | bytes 1769480 | tf_op jit(solution)/shard_map/ppermute | solution.py:172
  0.7 1.7 %collective-permute-start.1 = (s32[2,128]{1,0:T(2,128)S(1)}, s32[2,128]{1,0:T(2,128)S(1)}, u32[]{:S(2)}, u32[]{:S(2)}) collective-permute-start(s32[2,128]{1,0:T(2,128)S(1)} %bitcast.5), channel_id=1, source_target_pairs={{0,1},{1,0},{2,3},{3,2},{4,5},{5,4},{6,7},{7,6},{8,9},{9,8},{10,11... | collective-permute-start | bytes 3080 | tf_op jit(solution)/shard_map/ppermute | solution.py:172
  1.2 1.1 %copy-start = (f32[1,1,128,1152]{3,2,1,0:T(8,128)S(1)}, f32[1,1,128,1152]{3,2,1,0:T(8,128)}, u32[]{:S(2)}) copy-start(f32[1,1,128,1152]{3,2,1,0:T(8,128)} %param.2) | copy-start | bytes 1769476
  3.9 8.9 %collective-permute-start.2 = (bf16[32,1152]{1,0:T(8,128)(2,1)S(1)}, bf16[32,1152]{1,0:T(8,128)(2,1)S(1)}, u32[]{:S(2)}, u32[]{:S(2)}) collective-permute-start(bf16[32,1152]{1,0:T(8,128)(2,1)S(1)} %get-tuple-element.21), channel_id=1, source_target_pairs={{0,14},{1,13},{2,12},{3,15},{4,10},{5,9},{6,8},{7,11},{8,6},{9,5},... | collective-permute-start | bytes 221192 | tf_op jit(solution)/shard_map/ppermute | solution.py:181
  9.8 5.8 %collective-permute-start.3 = (bf16[32,1152]{1,0:T(8,128)(2,1)S(1)}, bf16[32,1152]{1,0:T(8,128)(2,1)S(1)}, u32[]{:S(2)}, u32[]{:S(2)}) collective-permute-start(bf16[32,1152]{1,0:T(8,128)(2,1)S(1)} %get-tuple-element.22), channel_id=1, source_target_pairs={{0,8},{1,11},{2,10},{3,9},{4,12},{5,15},{6,14},{7,13},{8,0},{9,3},... | collective-permute-start | bytes 221192 | tf_op jit(solution)/shard_map/ppermute | solution.py:181
  9.8 6.8 %collective-permute-start.4 = (bf16[32,1152]{1,0:T(8,128)(2,1)S(1)}, bf16[32,1152]{1,0:T(8,128)(2,1)S(1)}, u32[]{:S(2)}, u32[]{:S(2)}) collective-permute-start(bf16[32,1152]{1,0:T(8,128)(2,1)S(1)} %get-tuple-element.23), channel_id=1, source_target_pairs={{0,6},{1,5},{2,4},{3,7},{4,2},{5,1},{6,0},{7,3},{8,14},{9,13},{10,... | collective-permute-start | bytes 221192 | tf_op jit(solution)/shard_map/ppermute | solution.py:181
  10.4 6.1 %collective-permute-start.5 = (bf16[32,1152]{1,0:T(8,128)(2,1)S(1)}, bf16[32,1152]{1,0:T(8,128)(2,1)S(1)}, u32[]{:S(2)}, u32[]{:S(2)}) collective-permute-start(bf16[32,1152]{1,0:T(8,128)(2,1)S(1)} %get-tuple-element.24), channel_id=1, source_target_pairs={{0,0},{1,3},{2,2},{3,1},{4,4},{5,7},{6,6},{7,5},{8,8},{9,11},{10,1... | collective-permute-start | bytes 221192 | tf_op jit(solution)/shard_map/ppermute | solution.py:181
  12.8 4.2 %collective-permute-start.6 = (bf16[32,1152]{1,0:T(8,128)(2,1)S(1)}, bf16[32,1152]{1,0:T(8,128)(2,1)S(1)}, u32[]{:S(2)}, u32[]{:S(2)}) collective-permute-start(bf16[32,1152]{1,0:T(8,128)(2,1)S(1)} %collective-permute-done.2.refs_0_), channel_id=1, source_target_pairs={{0,1},{1,0},{2,3},{3,2},{4,5},{5,4},{6,7},{7,6},{8,9},{9,8},{10,11... | collective-permute-start | bytes 221192 | tf_op jit(solution)/shard_map/ppermute | solution.py:172
  15.6 1.5 %collective-permute-start.7 = (bf16[32,1152]{1,0:T(8,128)(2,1)S(1)}, bf16[32,1152]{1,0:T(8,128)(2,1)S(1)}, u32[]{:S(2)}, u32[]{:S(2)}) collective-permute-start(bf16[32,1152]{1,0:T(8,128)(2,1)S(1)} %collective-permute-done.3.refs_1_), channel_id=1, source_target_pairs={{0,1},{1,0},{2,3},{3,2},{4,5},{5,4},{6,7},{7,6},{8,9},{9,8},{10,11... | collective-permute-start | bytes 221192 | tf_op jit(solution)/shard_map/ppermute | solution.py:172
  16.6 1.3 %collective-permute-start.8 = (bf16[32,1152]{1,0:T(8,128)(2,1)S(1)}, bf16[32,1152]{1,0:T(8,128)(2,1)S(1)}, u32[]{:S(2)}, u32[]{:S(2)}) collective-permute-start(bf16[32,1152]{1,0:T(8,128)(2,1)S(1)} %collective-permute-done.4.refs_2_), channel_id=1, source_target_pairs={{0,1},{1,0},{2,3},{3,2},{4,5},{5,4},{6,7},{7,6},{8,9},{9,8},{10,11... | collective-permute-start | bytes 221192 | tf_op jit(solution)/shard_map/ppermute | solution.py:172
  16.6 1.4 %collective-permute-start.9 = (bf16[32,1152]{1,0:T(8,128)(2,1)S(1)}, bf16[32,1152]{1,0:T(8,128)(2,1)S(1)}, u32[]{:S(2)}, u32[]{:S(2)}) collective-permute-start(bf16[32,1152]{1,0:T(8,128)(2,1)S(1)} %collective-permute-done.5.refs_3_), channel_id=1, source_target_pairs={{0,1},{1,0},{2,3},{3,2},{4,5},{5,4},{6,7},{7,6},{8,9},{9,8},{10,11... | collective-permute-start | bytes 221192 | tf_op jit(solution)/shard_map/ppermute | solution.py:172
  19.2 7.7 %collective-permute-start.10 = (bf16[32,1152]{1,0:T(8,128)(2,1)S(1)}, bf16[32,1152]{1,0:T(8,128)(2,1)S(1)}, u32[]{:S(2)}, u32[]{:S(2)}) collective-permute-start(bf16[32,1152]{1,0:T(8,128)(2,1)S(1)} %get-tuple-element.25), channel_id=1, source_target_pairs={{0,14},{1,13},{2,12},{3,15},{4,10},{5,9},{6,8},{7,11},{8,6},{9,5},... | collective-permute-start | bytes 221192 | tf_op jit(solution)/shard_map/ppermute | solution.py:181
  21.9 6.9 %collective-permute-start.11 = (bf16[32,1152]{1,0:T(8,128)(2,1)S(1)}, bf16[32,1152]{1,0:T(8,128)(2,1)S(1)}, u32[]{:S(2)}, u32[]{:S(2)}) collective-permute-start(bf16[32,1152]{1,0:T(8,128)(2,1)S(1)} %get-tuple-element.26), channel_id=1, source_target_pairs={{0,8},{1,11},{2,10},{3,9},{4,12},{5,15},{6,14},{7,13},{8,0},{9,3},... | collective-permute-start | bytes 221192 | tf_op jit(solution)/shard_map/ppermute | solution.py:181
  21.9 7.1 %collective-permute-start.12 = (bf16[32,1152]{1,0:T(8,128)(2,1)S(1)}, bf16[32,1152]{1,0:T(8,128)(2,1)S(1)}, u32[]{:S(2)}, u32[]{:S(2)}) collective-permute-start(bf16[32,1152]{1,0:T(8,128)(2,1)S(1)} %get-tuple-element.27), channel_id=1, source_target_pairs={{0,6},{1,5},{2,4},{3,7},{4,2},{5,1},{6,0},{7,3},{8,14},{9,13},{10,... | collective-permute-start | bytes 221192 | tf_op jit(solution)/shard_map/ppermute | solution.py:181
  24.6 4.8 %collective-permute-start.13 = (bf16[32,1152]{1,0:T(8,128)(2,1)S(1)}, bf16[32,1152]{1,0:T(8,128)(2,1)S(1)}, u32[]{:S(2)}, u32[]{:S(2)}) collective-permute-start(bf16[32,1152]{1,0:T(8,128)(2,1)S(1)} %get-tuple-element.28), channel_id=1, source_target_pairs={{0,0},{1,3},{2,2},{3,1},{4,4},{5,7},{6,6},{7,5},{8,8},{9,11},{10,1... | collective-permute-start | bytes 221192 | tf_op jit(solution)/shard_map/ppermute | solution.py:181
  27.0 2.6 %collective-permute-start.14 = (bf16[32,1152]{1,0:T(8,128)(2,1)S(1)}, bf16[32,1152]{1,0:T(8,128)(2,1)S(1)}, u32[]{:S(2)}, u32[]{:S(2)}) collective-permute-start(bf16[32,1152]{1,0:T(8,128)(2,1)S(1)} %collective-permute-done.10.refs_0_), channel_id=1, source_target_pairs={{0,1},{1,0},{2,3},{3,2},{4,5},{5,4},{6,7},{7,6},{8,9},{9,8},{10,11... | collective-permute-start | bytes 221192 | tf_op jit(solution)/shard_map/ppermute | solution.py:172
  28.8 1.3 %collective-permute-start.15 = (bf16[32,1152]{1,0:T(8,128)(2,1)S(1)}, bf16[32,1152]{1,0:T(8,128)(2,1)S(1)}, u32[]{:S(2)}, u32[]{:S(2)}) collective-permute-start(bf16[32,1152]{1,0:T(8,128)(2,1)S(1)} %collective-permute-done.11.refs_1_), channel_id=1, source_target_pairs={{0,1},{1,0},{2,3},{3,2},{4,5},{5,4},{6,7},{7,6},{8,9},{9,8},{10,11... | collective-permute-start | bytes 221192 | tf_op jit(solution)/shard_map/ppermute | solution.py:172
  29.0 1.3 %collective-permute-start.16 = (bf16[32,1152]{1,0:T(8,128)(2,1)S(1)}, bf16[32,1152]{1,0:T(8,128)(2,1)S(1)}, u32[]{:S(2)}, u32[]{:S(2)}) collective-permute-start(bf16[32,1152]{1,0:T(8,128)(2,1)S(1)} %collective-permute-done.12.refs_2_), channel_id=1, source_target_pairs={{0,1},{1,0},{2,3},{3,2},{4,5},{5,4},{6,7},{7,6},{8,9},{9,8},{10,11... | collective-permute-start | bytes 221192 | tf_op jit(solution)/shard_map/ppermute | solution.py:172
  29.4 1.3 %collective-permute-start.17 = (bf16[32,1152]{1,0:T(8,128)(2,1)S(1)}, bf16[32,1152]{1,0:T(8,128)(2,1)S(1)}, u32[]{:S(2)}, u32[]{:S(2)}) collective-permute-start(bf16[32,1152]{1,0:T(8,128)(2,1)S(1)} %collective-permute-done.13.refs_3_), channel_id=1, source_target_pairs={{0,1},{1,0},{2,3},{3,2},{4,5},{5,4},{6,7},{7,6},{8,9},{9,8},{10,11... | collective-permute-start | bytes 221192 | tf_op jit(solution)/shard_map/ppermute | solution.py:172
where the time goes:
time: 32.7 us; the launch traced here: 32.5 us
  starting transfers between devices  15.4 us (47%)
  waiting for transfers between devices  11 us (34%)
  Pallas kernels  4.8 us (15%)
  local copies, waits for them, and re-layouts  1.25 us (4%)
    ppermute x8, starting transfers between devices, send(): return lax.ppermute(values, ('owner', 'sub', 'pair'), pairs)  13.1 us
    ppermute x8, waiting for transfers between devices, send(): return lax.ppermute(values, ('owner', 'sub', 'pair'), pairs)  9.05 us
    pallas_call x5, Pallas kernels, call(): pl.pallas_call(kernel, out_shape=out, in_specs=[pl.BlockSpec(memory_space...  4.8 us
    ppermute x10, starting transfers between devices, swap_pair(): return lax.ppermute(values, 'pair', [(0, 1), (1, 0)])  2.23 us
    ppermute x10, waiting for transfers between devices, swap_pair(): return lax.ppermute(values, 'pair', [(0, 1), (1, 0)])  1.98 us
    unnamed x4, local copies, waits for them, and re-layouts  1.25 us
  transfers between devices with their start and end apart: 18, of which 10 were waited for; matrix products, arithmetic and copies ran while one was open for 0% of the time, Pallas kernels for 1%

commit v1 on v0

--- a/solution.py
+++ b/solution.py
@@ -107,7 +107,11 @@
         keys = jnp.concatenate([heads, tails], axis=1)
         flags = live.astype(bf16)
         rough = jnp.concatenate([ref[...] for ref in blocks], axis=0)
-        scores = lax.dot_general(rough, rough, (((1,), (1,)), ((), ())), preferred_element_type=f32)
+        cut = width // (4 * LANES) * 2 * LANES + LANES
+        scores = sum(
+            lax.dot_general(part, part, (((1,), (1,)), ((), ())), preferred_element_type=f32)
+            for part in (rough[:, :cut], rough[:, cut:])
+        )
         _, core = here()
         share, _ = arrival(clusters, most, rows, iota((total_rows, 1), 0))
         slot = jnp.dot(ahead_ref[...], flags, preferred_element_type=f32)

time: 32.7 us -> 32.7 us (level)
  no operation moved by 1% of the time
where the time goes in v1:
time: 32.7 us; the launch traced here: 32.5 us
  starting transfers between devices  15.4 us (47%)
  waiting for transfers between devices  11 us (34%)
  Pallas kernels  4.79 us (15%)
  local copies, waits for them, and re-layouts  1.25 us (4%)
    ppermute x8, starting transfers between devices, send(): return lax.ppermute(values, ('owner', 'sub', 'pair'), pairs)  13.1 us
    ppermute x8, waiting for transfers between devices, send(): return lax.ppermute(values, ('owner', 'sub', 'pair'), pairs)  9.05 us
    pallas_call x5, Pallas kernels, call(): pl.pallas_call(kernel, out_shape=out, in_specs=[pl.BlockSpec(memory_space...  4.79 us
    ppermute x10, starting transfers between devices, swap_pair(): return lax.ppermute(values, 'pair', [(0, 1), (1, 0)])  2.22 us
    ppermute x10, waiting for transfers between devices, swap_pair(): return lax.ppermute(values, 'pair', [(0, 1), (1, 0)])  1.99 us
    unnamed x4, local copies, waits for them, and re-layouts  1.25 us
  transfers between devices with their start and end apart: 18, of which 10 were waited for; matrix products, arithmetic and copies ran while one was open for 0% of the time, Pallas kernels for 1%

profile of v1, /device:TPU:0, one launch (start us, length us, event | category | flops | bytes accessed | tf_op | source)
XLA Modules:
  0.0 32.5 jit_solution(6605867914780664384)
XLA Ops:
  0.0 0.0 copy-start.1
  0.0 0.5 %collective-permute-start = (f32[128,1152]{1,0:T(8,128)}, f32[128,1152]{1,0:T(8,128)S(1)}, u32[]{:S(2)}, u32[]{:S(2)}) collective-permute-start(f32[128,1152]{1,0:T(8,128)} %bitcast.3), channel_id=1, source_target_pairs={{0,1},{1,0},{2,3},{3,2},{4,5},{5,4},{6,7},{7,6},{8,9},{9,8},{10,11... | collective-permute-start | bytes 1769480 | tf_op jit(solution)/shard_map/ppermute | solution.py:176
  0.5 0.2 copy-done.1
  0.7 0.5 %collective-permute-start.1 = (s32[2,128]{1,0:T(2,128)S(1)}, s32[2,128]{1,0:T(2,128)S(1)}, u32[]{:S(2)}, u32[]{:S(2)}) collective-permute-start(s32[2,128]{1,0:T(2,128)S(1)} %bitcast.5), channel_id=1, source_target_pairs={{0,1},{1,0},{2,3},{3,2},{4,5},{5,4},{6,7},{7,6},{8,9},{9,8},{10,11... | collective-permute-start | bytes 3080 | tf_op jit(solution)/shard_map/ppermute | solution.py:176
  1.2 0.0 copy-start
  1.2 1.1 %copy-done = f32[1,1,128,1152]{3,2,1,0:T(8,128)S(1)} copy-done((f32[1,1,128,1152]{3,2,1,0:T(8,128)S(1)}, f32[1,1,128,1152]{3,2,1,0:T(8,128)}, u32[]{:S(2)}) %copy-start) | copy-done | bytes 589848
  2.2 0.2 shard_map.28
  2.4 0.0 collective-permute-done.1.refs_1_.refs_3_
  2.4 0.3 shard_map.29
  2.7 0.0 collective-permute-done.refs_2_
  2.7 1.2 %shard_map.30 = (bf16[32,1152]{1,0:T(8,128)(2,1)S(1)}, bf16[32,1152]{1,0:T(8,128)(2,1)S(1)}, bf16[32,1152]{1,0:T(8,128)(2,1)S(1)}, bf16[32,1152]{1,0:T(8,128)(2,1)S(1)}) custom-call(bf16[128,1152]{1,0:T(8,128)(2,1)S(1)} %get-tuple-element.17.refs_0_, bf16[128,128]{1,0:T(8,128)(2,1)S(1)} %get-tuple-element.18.refs_1_, ...), custom_call_target="tpu_custom_call" | custom-call | tf_op jit(solution)/shard_map/pallas_call | solution.py:165
  3.9 5.9 %collective-permute-start.2 = (bf16[32,1152]{1,0:T(8,128)(2,1)S(1)}, bf16[32,1152]{1,0:T(8,128)(2,1)S(1)}, u32[]{:S(2)}, u32[]{:S(2)}) collective-permute-start(bf16[32,1152]{1,0:T(8,128)(2,1)S(1)} %get-tuple-element.21), channel_id=1, source_target_pairs={{0,14},{1,13},{2,12},{3,15},{4,10},{5,9},{6,8},{7,11},{8,6},{9,5},... | collective-permute-start | bytes 221192 | tf_op jit(solution)/shard_map/ppermute | solution.py:185
  9.8 0.0 collective-permute-start.3
  9.8 0.6 %collective-permute-start.4 = (bf16[32,1152]{1,0:T(8,128)(2,1)S(1)}, bf16[32,1152]{1,0:T(8,128)(2,1)S(1)}, u32[]{:S(2)}, u32[]{:S(2)}) collective-permute-start(bf16[32,1152]{1,0:T(8,128)(2,1)S(1)} %get-tuple-element.23), channel_id=1, source_target_pairs={{0,6},{1,5},{2,4},{3,7},{4,2},{5,1},{6,0},{7,3},{8,14},{9,13},{10,... | collective-permute-start | bytes 221192 | tf_op jit(solution)/shard_map/ppermute | solution.py:185
  10.4 0.7 %collective-permute-start.5 = (bf16[32,1152]{1,0:T(8,128)(2,1)S(1)}, bf16[32,1152]{1,0:T(8,128)(2,1)S(1)}, u32[]{:S(2)}, u32[]{:S(2)}) collective-permute-start(bf16[32,1152]{1,0:T(8,128)(2,1)S(1)} %get-tuple-element.24), channel_id=1, source_target_pairs={{0,0},{1,3},{2,2},{3,1},{4,4},{5,7},{6,6},{7,5},{8,8},{9,11},{10,1... | collective-permute-start | bytes 221192 | tf_op jit(solution)/shard_map/ppermute | solution.py:185
  11.1 1.8 %collective-permute-done.2.refs_0_ = bf16[32,1152]{1,0:T(8,128)(2,1)S(1)} collective-permute-done((bf16[32,1152]{1,0:T(8,128)(2,1)S(1)}, bf16[32,1152]{1,0:T(8,128)(2,1)S(1)}, u32[]{:S(2)}, u32[]{:S(2)}) %collective-permute-start.2) | collective-permute-done | bytes 73760 | tf_op jit(solution)/shard_map/ppermute | solution.py:185
  12.8 0.0 collective-permute-start.6
  12.9 2.8 %collective-permute-done.3.refs_1_ = bf16[32,1152]{1,0:T(8,128)(2,1)S(1)} collective-permute-done((bf16[32,1152]{1,0:T(8,128)(2,1)S(1)}, bf16[32,1152]{1,0:T(8,128)(2,1)S(1)}, u32[]{:S(2)}, u32[]{:S(2)}) %collective-permute-start.3) | collective-permute-done | bytes 73760 | tf_op jit(solution)/shard_map/ppermute | solution.py:185
  15.6 0.0 collective-permute-start.7
  15.6 0.9 %collective-permute-done.4.refs_2_ = bf16[32,1152]{1,0:T(8,128)(2,1)S(1)} collective-permute-done((bf16[32,1152]{1,0:T(8,128)(2,1)S(1)}, bf16[32,1152]{1,0:T(8,128)(2,1)S(1)}, u32[]{:S(2)}, u32[]{:S(2)}) %collective-permute-start.4) | collective-permute-done | bytes 73760 | tf_op jit(solution)/shard_map/ppermute | solution.py:185
  16.6 0.0 collective-permute-start.8
  16.6 0.0 collective-permute-done.5.refs_3_
  16.6 0.5 %collective-permute-start.9 = (bf16[32,1152]{1,0:T(8,128)(2,1)S(1)}, bf16[32,1152]{1,0:T(8,128)(2,1)S(1)}, u32[]{:S(2)}, u32[]{:S(2)}) collective-permute-start(bf16[32,1152]{1,0:T(8,128)(2,1)S(1)} %collective-permute-done.5.refs_3_), channel_id=1, source_target_pairs={{0,1},{1,0},{2,3},{3,2},{4,5},{5,4},{6,7},{7,6},{8,9},{9,8},{10,11... | collective-permute-start | bytes 221192 | tf_op jit(solution)/shard_map/ppermute | solution.py:176
  17.1 0.0 collective-permute-done.6.refs_4_
  17.1 0.0 collective-permute-done.7.refs_5_
  17.1 0.7 %collective-permute-done.8.refs_6_ = bf16[32,1152]{1,0:T(8,128)(2,1)S(1)} collective-permute-done((bf16[32,1152]{1,0:T(8,128)(2,1)S(1)}, bf16[32,1152]{1,0:T(8,128)(2,1)S(1)}, u32[]{:S(2)}, u32[]{:S(2)}) %collective-permute-start.8) | collective-permute-done | bytes 73760 | tf_op jit(solution)/shard_map/ppermute | solution.py:176
  17.8 0.2 collective-permute-done.9.refs_7_
  18.0 1.2 %shard_map.31 = (bf16[32,1152]{1,0:T(8,128)(2,1)S(1)}, bf16[32,1152]{1,0:T(8,128)(2,1)S(1)}, bf16[32,1152]{1,0:T(8,128)(2,1)S(1)}, bf16[32,1152]{1,0:T(8,128)(2,1)S(1)}) custom-call(bf16[32,1152]{1,0:T(8,128)(2,1)S(1)} %collective-permute-done.2.refs_0_, bf16[32,1152]{1,0:T(8,128)(2,1)S(1)} %collective-permute-done.3.refs_1_, ...), custom_call_target="tpu_custom_call" | custom-call | tf_op jit(solution)/shard_map/pallas_call | solution.py:165
  19.2 2.7 %collective-permute-start.10 = (bf16[32,1152]{1,0:T(8,128)(2,1)S(1)}, bf16[32,1152]{1,0:T(8,128)(2,1)S(1)}, u32[]{:S(2)}, u32[]{:S(2)}) collective-permute-start(bf16[32,1152]{1,0:T(8,128)(2,1)S(1)} %get-tuple-element.25), channel_id=1, source_target_pairs={{0,14},{1,13},{2,12},{3,15},{4,10},{5,9},{6,8},{7,11},{8,6},{9,5},... | collective-permute-start | bytes 221192 | tf_op jit(solution)/shard_map/ppermute | solution.py:185
  21.9 0.0 collective-permute-start.11
  21.9 2.7 %collective-permute-start.12 = (bf16[32,1152]{1,0:T(8,128)(2,1)S(1)}, bf16[32,1152]{1,0:T(8,128)(2,1)S(1)}, u32[]{:S(2)}, u32[]{:S(2)}) collective-permute-start(bf16[32,1152]{1,0:T(8,128)(2,1)S(1)} %get-tuple-element.27), channel_id=1, source_target_pairs={{0,6},{1,5},{2,4},{3,7},{4,2},{5,1},{6,0},{7,3},{8,14},{9,13},{10,... | collective-permute-start | bytes 221192 | tf_op jit(solution)/shard_map/ppermute | solution.py:185
  24.6 0.7 %collective-permute-start.13 = (bf16[32,1152]{1,0:T(8,128)(2,1)S(1)}, bf16[32,1152]{1,0:T(8,128)(2,1)S(1)}, u32[]{:S(2)}, u32[]{:S(2)}) collective-permute-start(bf16[32,1152]{1,0:T(8,128)(2,1)S(1)} %get-tuple-element.28), channel_id=1, source_target_pairs={{0,0},{1,3},{2,2},{3,1},{4,4},{5,7},{6,6},{7,5},{8,8},{9,11},{10,1... | collective-permute-start | bytes 221192 | tf_op jit(solution)/shard_map/ppermute | solution.py:185
  25.2 1.7 %collective-permute-done.10.refs_0_ = bf16[32,1152]{1,0:T(8,128)(2,1)S(1)} collective-permute-done((bf16[32,1152]{1,0:T(8,128)(2,1)S(1)}, bf16[32,1152]{1,0:T(8,128)(2,1)S(1)}, u32[]{:S(2)}, u32[]{:S(2)}) %collective-permute-start.10) | collective-permute-done | bytes 73760 | tf_op jit(solution)/shard_map/ppermute | solution.py:185
  26.9 0.0 collective-permute-start.14
  27.0 1.9 %collective-permute-done.11.refs_1_ = bf16[32,1152]{1,0:T(8,128)(2,1)S(1)} collective-permute-done((bf16[32,1152]{1,0:T(8,128)(2,1)S(1)}, bf16[32,1152]{1,0:T(8,128)(2,1)S(1)}, u32[]{:S(2)}, u32[]{:S(2)}) %collective-permute-start.11) | collective-permute-done | bytes 73760 | tf_op jit(solution)/shard_map/ppermute | solution.py:185
  28.8 0.2 collective-permute-start.15
  29.0 0.0 collective-permute-done.12.refs_2_
  29.0 0.3 collective-permute-start.16
  29.4 0.0 collective-permute-done.13.refs_3_
  29.4 0.2 collective-permute-start.17
  29.6 0.0 collective-permute-done.14.refs_4_
  29.6 0.5 %collective-permute-done.15.refs_5_ = bf16[32,1152]{1,0:T(8,128)(2,1)S(1)} collective-permute-done((bf16[32,1152]{1,0:T(8,128)(2,1)S(1)}, bf16[32,1152]{1,0:T(8,128)(2,1)S(1)}, u32[]{:S(2)}, u32[]{:S(2)}) %collective-permute-start.15) | collective-permute-done | bytes 73760 | tf_op jit(solution)/shard_map/ppermute | solution.py:176
  30.1 0.2 collective-permute-done.16.refs_6_
  30.3 0.3 collective-permute-done.17.refs_7_
  30.6 1.9 %shard_map.32 = f32[128,1152]{1,0:T(8,128)} custom-call(bf16[32,1152]{1,0:T(8,128)(2,1)S(1)} %collective-permute-done.10.refs_0_, bf16[32,1152]{1,0:T(8,128)(2,1)S(1)} %collective-permute-done.11.refs_1_, bf16[32,1152]{1,0:T(8,128)(2,1)S(1)} %collective-permute-done.12.refs_2_, bf16[32,1152]{1,0:T(8,128)(2,1)S(1)} %collective-permute-done.13.refs_3_, ...), custom_call_target="tpu_custom_call" | custom-call | tf_op jit(solution)/shard_map/pallas_call | solution.py:165
Async XLA Ops:
  0.0 0.7 %copy-start.1 = (s32[2,1,1,128]{3,2,1,0:T(1,128)S(1)}, s32[2,1,1,128]{3,2,1,0:T(1,128)}, u32[]{:S(2)}) copy-start(s32[2,1,1,128]{3,2,1,0:T(1,128)} %param.3) | copy-start | bytes 3076
  0.0 2.7 %collective-permute-start = (f32[128,1152]{1,0:T(8,128)}, f32[128,1152]{1,0:T(8,128)S(1)}, u32[]{:S(2)}, u32[]{:S(2)}) collective-permute-start(f32[128,1152]{1,0:T(8,128)} %bitcast.3), channel_id=1, source_target_pairs={{0,1},{1,0},{2,3},{3,2},{4,5},{5,4},{6,7},{7,6},{8,9},{9,8},{10,11... | collective-permute-start | bytes 1769480 | tf_op jit(solution)/shard_map/ppermute | solution.py:176
  0.7 1.7 %collective-permute-start.1 = (s32[2,128]{1,0:T(2,128)S(1)}, s32[2,128]{1,0:T(2,128)S(1)}, u32[]{:S(2)}, u32[]{:S(2)}) collective-permute-start(s32[2,128]{1,0:T(2,128)S(1)} %bitcast.5), channel_id=1, source_target_pairs={{0,1},{1,0},{2,3},{3,2},{4,5},{5,4},{6,7},{7,6},{8,9},{9,8},{10,11... | collective-permute-start | bytes 3080 | tf_op jit(solution)/shard_map/ppermute | solution.py:176
  1.2 1.1 %copy-start = (f32[1,1,128,1152]{3,2,1,0:T(8,128)S(1)}, f32[1,1,128,1152]{3,2,1,0:T(8,128)}, u32[]{:S(2)}) copy-start(f32[1,1,128,1152]{3,2,1,0:T(8,128)} %param.2) | copy-start | bytes 1769476
  3.9 8.9 %collective-permute-start.2 = (bf16[32,1152]{1,0:T(8,128)(2,1)S(1)}, bf16[32,1152]{1,0:T(8,128)(2,1)S(1)}, u32[]{:S(2)}, u32[]{:S(2)}) collective-permute-start(bf16[32,1152]{1,0:T(8,128)(2,1)S(1)} %get-tuple-element.21), channel_id=1, source_target_pairs={{0,14},{1,13},{2,12},{3,15},{4,10},{5,9},{6,8},{7,11},{8,6},{9,5},... | collective-permute-start | bytes 221192 | tf_op jit(solution)/shard_map/ppermute | solution.py:185
  9.8 5.8 %collective-permute-start.3 = (bf16[32,1152]{1,0:T(8,128)(2,1)S(1)}, bf16[32,1152]{1,0:T(8,128)(2,1)S(1)}, u32[]{:S(2)}, u32[]{:S(2)}) collective-permute-start(bf16[32,1152]{1,0:T(8,128)(2,1)S(1)} %get-tuple-element.22), channel_id=1, source_target_pairs={{0,8},{1,11},{2,10},{3,9},{4,12},{5,15},{6,14},{7,13},{8,0},{9,3},... | collective-permute-start | bytes 221192 | tf_op jit(solution)/shard_map/ppermute | solution.py:185
  9.8 6.8 %collective-permute-start.4 = (bf16[32,1152]{1,0:T(8,128)(2,1)S(1)}, bf16[32,1152]{1,0:T(8,128)(2,1)S(1)}, u32[]{:S(2)}, u32[]{:S(2)}) collective-permute-start(bf16[32,1152]{1,0:T(8,128)(2,1)S(1)} %get-tuple-element.23), channel_id=1, source_target_pairs={{0,6},{1,5},{2,4},{3,7},{4,2},{5,1},{6,0},{7,3},{8,14},{9,13},{10,... | collective-permute-start | bytes 221192 | tf_op jit(solution)/shard_map/ppermute | solution.py:185
  10.4 6.1 %collective-permute-start.5 = (bf16[32,1152]{1,0:T(8,128)(2,1)S(1)}, bf16[32,1152]{1,0:T(8,128)(2,1)S(1)}, u32[]{:S(2)}, u32[]{:S(2)}) collective-permute-start(bf16[32,1152]{1,0:T(8,128)(2,1)S(1)} %get-tuple-element.24), channel_id=1, source_target_pairs={{0,0},{1,3},{2,2},{3,1},{4,4},{5,7},{6,6},{7,5},{8,8},{9,11},{10,1... | collective-permute-start | bytes 221192 | tf_op jit(solution)/shard_map/ppermute | solution.py:185
  12.8 4.2 %collective-permute-start.6 = (bf16[32,1152]{1,0:T(8,128)(2,1)S(1)}, bf16[32,1152]{1,0:T(8,128)(2,1)S(1)}, u32[]{:S(2)}, u32[]{:S(2)}) collective-permute-start(bf16[32,1152]{1,0:T(8,128)(2,1)S(1)} %collective-permute-done.2.refs_0_), channel_id=1, source_target_pairs={{0,1},{1,0},{2,3},{3,2},{4,5},{5,4},{6,7},{7,6},{8,9},{9,8},{10,11... | collective-permute-start | bytes 221192 | tf_op jit(solution)/shard_map/ppermute | solution.py:176
  15.6 1.5 %collective-permute-start.7 = (bf16[32,1152]{1,0:T(8,128)(2,1)S(1)}, bf16[32,1152]{1,0:T(8,128)(2,1)S(1)}, u32[]{:S(2)}, u32[]{:S(2)}) collective-permute-start(bf16[32,1152]{1,0:T(8,128)(2,1)S(1)} %collective-permute-done.3.refs_1_), channel_id=1, source_target_pairs={{0,1},{1,0},{2,3},{3,2},{4,5},{5,4},{6,7},{7,6},{8,9},{9,8},{10,11... | collective-permute-start | bytes 221192 | tf_op jit(solution)/shard_map/ppermute | solution.py:176
  16.6 1.3 %collective-permute-start.8 = (bf16[32,1152]{1,0:T(8,128)(2,1)S(1)}, bf16[32,1152]{1,0:T(8,128)(2,1)S(1)}, u32[]{:S(2)}, u32[]{:S(2)}) collective-permute-start(bf16[32,1152]{1,0:T(8,128)(2,1)S(1)} %collective-permute-done.4.refs_2_), channel_id=1, source_target_pairs={{0,1},{1,0},{2,3},{3,2},{4,5},{5,4},{6,7},{7,6},{8,9},{9,8},{10,11... | collective-permute-start | bytes 221192 | tf_op jit(solution)/shard_map/ppermute | solution.py:176
  16.6 1.4 %collective-permute-start.9 = (bf16[32,1152]{1,0:T(8,128)(2,1)S(1)}, bf16[32,1152]{1,0:T(8,128)(2,1)S(1)}, u32[]{:S(2)}, u32[]{:S(2)}) collective-permute-start(bf16[32,1152]{1,0:T(8,128)(2,1)S(1)} %collective-permute-done.5.refs_3_), channel_id=1, source_target_pairs={{0,1},{1,0},{2,3},{3,2},{4,5},{5,4},{6,7},{7,6},{8,9},{9,8},{10,11... | collective-permute-start | bytes 221192 | tf_op jit(solution)/shard_map/ppermute | solution.py:176
  19.2 7.7 %collective-permute-start.10 = (bf16[32,1152]{1,0:T(8,128)(2,1)S(1)}, bf16[32,1152]{1,0:T(8,128)(2,1)S(1)}, u32[]{:S(2)}, u32[]{:S(2)}) collective-permute-start(bf16[32,1152]{1,0:T(8,128)(2,1)S(1)} %get-tuple-element.25), channel_id=1, source_target_pairs={{0,14},{1,13},{2,12},{3,15},{4,10},{5,9},{6,8},{7,11},{8,6},{9,5},... | collective-permute-start | bytes 221192 | tf_op jit(solution)/shard_map/ppermute | solution.py:185
  21.9 6.9 %collective-permute-start.11 = (bf16[32,1152]{1,0:T(8,128)(2,1)S(1)}, bf16[32,1152]{1,0:T(8,128)(2,1)S(1)}, u32[]{:S(2)}, u32[]{:S(2)}) collective-permute-start(bf16[32,1152]{1,0:T(8,128)(2,1)S(1)} %get-tuple-element.26), channel_id=1, source_target_pairs={{0,8},{1,11},{2,10},{3,9},{4,12},{5,15},{6,14},{7,13},{8,0},{9,3},... | collective-permute-start | bytes 221192 | tf_op jit(solution)/shard_map/ppermute | solution.py:185
  21.9 7.1 %collective-permute-start.12 = (bf16[32,1152]{1,0:T(8,128)(2,1)S(1)}, bf16[32,1152]{1,0:T(8,128)(2,1)S(1)}, u32[]{:S(2)}, u32[]{:S(2)}) collective-permute-start(bf16[32,1152]{1,0:T(8,128)(2,1)S(1)} %get-tuple-element.27), channel_id=1, source_target_pairs={{0,6},{1,5},{2,4},{3,7},{4,2},{5,1},{6,0},{7,3},{8,14},{9,13},{10,... | collective-permute-start | bytes 221192 | tf_op jit(solution)/shard_map/ppermute | solution.py:185
  24.6 4.8 %collective-permute-start.13 = (bf16[32,1152]{1,0:T(8,128)(2,1)S(1)}, bf16[32,1152]{1,0:T(8,128)(2,1)S(1)}, u32[]{:S(2)}, u32[]{:S(2)}) collective-permute-start(bf16[32,1152]{1,0:T(8,128)(2,1)S(1)} %get-tuple-element.28), channel_id=1, source_target_pairs={{0,0},{1,3},{2,2},{3,1},{4,4},{5,7},{6,6},{7,5},{8,8},{9,11},{10,1... | collective-permute-start | bytes 221192 | tf_op jit(solution)/shard_map/ppermute | solution.py:185
  26.9 2.6 %collective-permute-start.14 = (bf16[32,1152]{1,0:T(8,128)(2,1)S(1)}, bf16[32,1152]{1,0:T(8,128)(2,1)S(1)}, u32[]{:S(2)}, u32[]{:S(2)}) collective-permute-start(bf16[32,1152]{1,0:T(8,128)(2,1)S(1)} %collective-permute-done.10.refs_0_), channel_id=1, source_target_pairs={{0,1},{1,0},{2,3},{3,2},{4,5},{5,4},{6,7},{7,6},{8,9},{9,8},{10,11... | collective-permute-start | bytes 221192 | tf_op jit(solution)/shard_map/ppermute | solution.py:176
  28.8 1.3 %collective-permute-start.15 = (bf16[32,1152]{1,0:T(8,128)(2,1)S(1)}, bf16[32,1152]{1,0:T(8,128)(2,1)S(1)}, u32[]{:S(2)}, u32[]{:S(2)}) collective-permute-start(bf16[32,1152]{1,0:T(8,128)(2,1)S(1)} %collective-permute-done.11.refs_1_), channel_id=1, source_target_pairs={{0,1},{1,0},{2,3},{3,2},{4,5},{5,4},{6,7},{7,6},{8,9},{9,8},{10,11... | collective-permute-start | bytes 221192 | tf_op jit(solution)/shard_map/ppermute | solution.py:176
  29.0 1.3 %collective-permute-start.16 = (bf16[32,1152]{1,0:T(8,128)(2,1)S(1)}, bf16[32,1152]{1,0:T(8,128)(2,1)S(1)}, u32[]{:S(2)}, u32[]{:S(2)}) collective-permute-start(bf16[32,1152]{1,0:T(8,128)(2,1)S(1)} %collective-permute-done.12.refs_2_), channel_id=1, source_target_pairs={{0,1},{1,0},{2,3},{3,2},{4,5},{5,4},{6,7},{7,6},{8,9},{9,8},{10,11... | collective-permute-start | bytes 221192 | tf_op jit(solution)/shard_map/ppermute | solution.py:176
  29.4 1.3 %collective-permute-start.17 = (bf16[32,1152]{1,0:T(8,128)(2,1)S(1)}, bf16[32,1152]{1,0:T(8,128)(2,1)S(1)}, u32[]{:S(2)}, u32[]{:S(2)}) collective-permute-start(bf16[32,1152]{1,0:T(8,128)(2,1)S(1)} %collective-permute-done.13.refs_3_), channel_id=1, source_target_pairs={{0,1},{1,0},{2,3},{3,2},{4,5},{5,4},{6,7},{7,6},{8,9},{9,8},{10,11... | collective-permute-start | bytes 221192 | tf_op jit(solution)/shard_map/ppermute | solution.py:176
